TPU v7x, 32 devices: a whole 2x2x4 slice. The times are simulated.
32 devices in a mesh: px: 8 (over z, x), py: 4 (over y, core).
Axes of the slice: x: 2, y: 2, z: 4, core: 2. Of those that a mesh axis runs over, the one named last changes fastest.
Arguments:
- conserved: float32 [2, 2, 2, 2, 32, 32, 128], P(None, None, None, None, 'px', 'py'), may hold values from 0.075 to 36
- velocity: float32 [3, 3, 3, 3, 32, 32, 128], P(None, None, None, None, 'px', 'py'), may hold values from -6 to 6
- targets: float32 [2], replicated, may hold values from 0.5 to 2
- handoff_blocks: int32 [8, 32], P('px', 'py'), may hold values from 0 to 31, as said below
- handoff_owner: int32 [8, 32, 1], P('px', 'py'), may hold values from 0 to 3; in each aligned block of 8 rows (0 to 7, 8 to 15, ..., all dimensions but the last counted through in order) at most 4 rows name the same one
Outputs:
- fixed_state: float32 [2, 2, 2, 2, 32, 32, 128], P(None, None, None, None, 'px', 'py')
- handed: float32 [8, 64, 16, 128], P('px', 'py')
Inputs may be any that keep to these rules, and one draw needn't show every extreme that they name: `handoff_blocks`: within one device's 8 entries the column numbers are distinct; column b is the local zone column (b // 8, b % 8). `handoff_owner`: owners are indices along py within the same px group; at most 4 of one device's entries name the same owner, and in some device one owner is named exactly 4 times.
All inputs are finite; a program needn't handle non-finite values.
Results may differ from a plain program's by a relative error of at most 0.00035.
Values sent between devices are 32-bit elements; how exact they have to be, the bound alone decides.
No kernel may reach another device: no remote copies, remote signals or barrier semaphores. Data moves between devices by JAX's collectives and lax.ppermute only.
A program may use at most 64 MiB of HBM per device.

v0:
```python
import math
import jax
import jax.numpy as jnp
import numpy as np
from jax import lax
from jax.sharding import PartitionSpec as P

gamma_less = 0.4
force_step = 0.02
advect_step = 0.5
highest = lax.Precision.HIGHEST


def passed_along(x, axis, by):
    size = lax.axis_size(axis)
    pairs = [(i, i + by) for i in range(size) if 0 <= i + by < size]
    return lax.ppermute(x, axis, pairs)


def triple(factor_one, factor_two, factor_three):
    return np.kron(np.kron(factor_one, factor_two), factor_three)


def build_tables():
    offset = 0.5 / math.sqrt(3.0)
    gauss_nodes = np.array([0.5 - offset, 0.5 + offset])
    linear = np.stack([1.0 - gauss_nodes, gauss_nodes], 1)
    quadratic = np.stack(
        [
            2.0 * (gauss_nodes - 0.5) * (gauss_nodes - 1.0),
            -4.0 * gauss_nodes * (gauss_nodes - 1.0),
            2.0 * gauss_nodes * (gauss_nodes - 0.5),
        ],
        1,
    )
    slopes = np.stack(
        [4.0 * gauss_nodes - 3.0, 4.0 - 8.0 * gauss_nodes, 4.0 * gauss_nodes - 1.0], 1
    )
    line_mass = np.array([[1.0 / 3.0, 1.0 / 6.0], [1.0 / 6.0, 1.0 / 3.0]])
    line_inverse = np.array([[4.0, -2.0], [-2.0, 4.0]])
    line_drift = np.array([[-0.5, -0.5], [0.5, 0.5]])
    basis = triple(linear, linear, linear)
    gradient = np.stack(
        [
            triple(slopes, quadratic, quadratic),
            triple(quadratic, slopes, quadratic),
            triple(quadratic, quadratic, slopes),
        ],
        1,
    ).reshape(8, 81)
    inverse = triple(line_inverse, line_inverse, line_inverse)
    project = inverse @ basis.T / 8.0
    stiffness = np.stack(
        [
            triple(line_drift, line_mass, line_mass),
            triple(line_mass, line_drift, line_mass),
            triple(line_mass, line_mass, line_drift),
        ]
    )
    face_mass = np.kron(line_mass, line_mass)
    return tuple(
        (
            jnp.asarray(entry_table, jnp.float32)
            for entry_table in (basis, gradient, inverse, project, stiffness, face_mass)
        )
    )


def face_weight(fluxes, face_mass):
    layout = fluxes.shape
    grouped = fluxes.reshape(layout[0], 4, -1)
    return jnp.einsum("ab,fbn->fan", face_mass, grouped, precision=highest).reshape(layout)


def upwind(left_trace, right_trace, speeds, face_mass):
    fluxes = 0.5 * speeds * (left_trace + right_trace) + 0.5 * jnp.abs(speeds) * (
        left_trace - right_trace
    )
    return face_weight(fluxes, face_mass)


def lagrange_section(conserved, velocity, tables):
    basis, gradient, inverse, project, stiffness, face_mass = tables
    layout = conserved.shape
    zone_count = layout[4] * layout[5] * layout[6]
    fields = conserved.reshape(2, 8, zone_count)
    node_motion = velocity.reshape(81, zone_count)
    divergence = jnp.dot(gradient, node_motion, precision=highest)
    pressure = gamma_less * jnp.dot(basis, fields[1], precision=highest)
    energy = fields[1] - force_step * jnp.dot(project, pressure * divergence, precision=highest)
    lagrange = jnp.stack([fields[0], energy]).reshape(layout)
    mean_motion = jnp.sum(velocity.reshape(3, 27, layout[4], layout[5], layout[6]), axis=1) / 27.0
    padded = jnp.pad(mean_motion, ((0, 0), (0, 0), (0, 0), (1, 1)))
    relaxed = 0.25 * (padded[..., :-2] + 2.0 * mean_motion + padded[..., 2:])
    return (lagrange, mean_motion - relaxed)


def advect(lagrange, relative, x_faces, y_faces, tables):
    basis, gradient, inverse, project, stiffness, face_mass = tables
    layout = lagrange.shape
    zone_count = layout[4] * layout[5] * layout[6]
    flat_state = lagrange.reshape(2, 8, zone_count)
    volume = jnp.zeros_like(flat_state)
    for direction in range(3):
        volume = volume + jnp.einsum(
            "jk,fkn->fjn", stiffness[direction], flat_state, precision=highest
        ) * relative[direction].reshape(1, 1, zone_count)
    padded_z = jnp.pad(lagrange, ((0, 0),) * 6 + ((1, 1),))
    motion_z = jnp.pad(relative[2], ((0, 0), (0, 0), (1, 1)))
    flux_z = upwind(
        padded_z[:, :, :, 1, :, :, :-1],
        padded_z[:, :, :, 0, :, :, 1:],
        0.5 * (motion_z[..., :-1] + motion_z[..., 1:]),
        face_mass,
    )
    face_z = jnp.stack([-flux_z[..., :-1], flux_z[..., 1:]], axis=3)
    flux_x = upwind(x_faces[0], x_faces[1], x_faces[2], face_mass)
    face_x = jnp.stack([-flux_x[:, :, :, :-1], flux_x[:, :, :, 1:]], axis=1)
    flux_y = upwind(y_faces[0], y_faces[1], y_faces[2], face_mass)
    face_y = jnp.stack([-flux_y[:, :, :, :, :-1], flux_y[:, :, :, :, 1:]], axis=2)
    balance = volume - (face_x + face_y + face_z).reshape(2, 8, zone_count)
    remapped = flat_state + advect_step * jnp.einsum(
        "jk,fkn->fjn", inverse, balance, precision=highest
    )
    return remapped.reshape(layout)


def body(conserved, velocity, targets, handoff_blocks, handoff_owner):
    tables = build_tables()
    lagrange, relative = lagrange_section(conserved, velocity, tables)
    width_x = lagrange.shape[4]
    width_y = lagrange.shape[5]
    depth_z = lagrange.shape[6]
    count_px = lax.axis_size("px")
    count_py = lax.axis_size("py")
    total_zones = 8.0 * width_x * width_y * depth_z * count_px * count_py
    upper_x = jnp.concatenate(
        [lagrange[:, 1, :, :, -1].reshape((8, width_y, depth_z)), relative[0, -1][None]], axis=0
    )
    lower_x = jnp.concatenate(
        [lagrange[:, 0, :, :, 0].reshape((8, width_y, depth_z)), relative[0, 0][None]], axis=0
    )
    below_x = passed_along(upper_x, "px", 1)
    above_x = passed_along(lower_x, "px", -1)
    left_x = jnp.concatenate(
        [below_x[:8].reshape((2, 2, 2, 1, width_y, depth_z)), lagrange[:, 1]], axis=3
    )
    right_x = jnp.concatenate(
        [lagrange[:, 0], above_x[:8].reshape((2, 2, 2, 1, width_y, depth_z))], axis=3
    )
    motion_x = jnp.concatenate([below_x[8][None], relative[0], above_x[8][None]], axis=0)
    x_faces = (left_x, right_x, 0.5 * (motion_x[:-1] + motion_x[1:]))
    upper_y = jnp.concatenate(
        [lagrange[:, :, 1, :, :, -1].reshape((8, width_x, depth_z)), relative[1][:, -1][None]],
        axis=0,
    )
    lower_y = jnp.concatenate(
        [lagrange[:, :, 0, :, :, 0].reshape((8, width_x, depth_z)), relative[1][:, 0][None]], axis=0
    )
    below_y = passed_along(upper_y, "py", 1)
    above_y = passed_along(lower_y, "py", -1)
    left_y = jnp.concatenate(
        [below_y[:8].reshape((2, 2, 2, width_x, 1, depth_z)), lagrange[:, :, 1]], axis=4
    )
    right_y = jnp.concatenate(
        [lagrange[:, :, 0], above_y[:8].reshape((2, 2, 2, width_x, 1, depth_z))], axis=4
    )
    motion_y = jnp.concatenate([below_y[8][:, None], relative[1], above_y[8][:, None]], axis=1)
    y_faces = (left_y, right_y, 0.5 * (motion_y[:, :-1] + motion_y[:, 1:]))
    remapped = advect(lagrange, relative, x_faces, y_faces, tables)
    totals = lax.psum(jnp.sum(remapped.reshape(2, -1), axis=1), ("px", "py"))
    field_means = totals / total_zones
    fixed_state = remapped * (targets / field_means).reshape(2, 1, 1, 1, 1, 1, 1)
    entries = handoff_blocks.shape[1]
    capacity = max(2, 2 * entries // count_py)
    blocks = handoff_blocks[0]
    owners = handoff_owner[0, :, 0]
    onehot = (owners[:, None] == jnp.arange(count_py, dtype=jnp.int32)).astype(jnp.int32)
    earlier = jnp.cumsum(onehot, axis=0) - onehot
    slot_index = jnp.sum(onehot * earlier, axis=1)
    position = owners * capacity + slot_index
    placing = (
        position[None, :] == jnp.arange(count_py * capacity, dtype=jnp.int32)[:, None]
    ).astype(jnp.float32)
    columns = fixed_state.reshape((16, width_x * width_y, depth_z))
    picked = jnp.take(columns, blocks, axis=1)
    send_rows = jnp.einsum("sn,cnz->scz", placing, picked, precision=highest).reshape(
        (count_py, capacity, 16, depth_z)
    )
    received = lax.all_to_all(send_rows, "py", split_axis=0, concat_axis=0, tiled=True)
    handed = received.reshape((1, count_py * capacity, 16, depth_z))
    return (fixed_state, handed)


def solution(mesh):
    return jax.shard_map(
        body,
        mesh=mesh,
        in_specs=(
            P(None, None, None, None, "px", "py", None),
            P(None, None, None, None, "px", "py", None),
            P(),
            P("px", "py"),
            P("px", "py", None),
        ),
        out_specs=(P(None, None, None, None, "px", "py", None), P("px", "py", None, None)),
        check_vma=False,
    )
```

profile of v0, /device:TPU:0, one launch (start us, length us, event | category | flops | bytes accessed | tf_op | source)
XLA Modules:
  0.0 75.8 jit_solution(11837693475548157601)
XLA Ops:
  0.6 1.0 %fusion.62 = (f32[1,2,2,2,4,8,128]{6,5,4,3,2,1,0:T(8,128)S(1)}, f32[1,2,2,2,4,8,128]{6,5,4,3,2,1,0:T(8,128)S(1)}) fusion(f32[2,2,2,2,4,8,128]{6,5,4,3,2,1,0:T(8,128)} %param.11), kind=kLoop, calls=%fused_computation.139 | loop fusion | bytes 524288 | tf_op jit(solution)/shard_map/slice | solution.py:90
  1.7 1.5 %reshape.163 = f32[81,4096]{1,0:T(8,128)S(1)} reshape(f32[3,3,3,3,4,8,128]{6,5,4,3,2,1,0:T(8,128)} %param.12) | data formatting | bytes 2654208 | tf_op jit(solution)/shard_map/reshape | solution.py:87
  3.3 0.3 convolution_multiply_fusion.6
  3.5 0.8 %convolution_multiply_fusion.5 = f32[8,4096]{1,0:T(8,128)S(1)} fusion(f32[8,4096]{1,0:T(8,128)S(1)} %convolution_multiply_fusion.6, f32[8,81]{1,0:T(8,128)S(1)} %copy-done.8, f32[81,4096]{1,0:T(8,128)S(1)} %reshape.163), kind=kOutput, calls=%fused_computation.17 | convolution fusion | flops 31883264 | bytes 1591840 | tf_op jit(solution)/shard_map/dot_general | solution.py:88
  4.3 0.3 fusion.7
  4.6 0.1 reduce_sum.27
  4.7 0.1 fusion.46
  4.9 2.4 %collective-permute-start.2 = (f32[9,4,128]{2,1,0:T(4,128)S(1)}, f32[9,4,128]{2,1,0:T(4,128)S(1)}, u32[]{:S(2)}, u32[]{:S(2)}) collective-permute-start(f32[9,4,128]{2,1,0:T(4,128)S(1)} %pad_maximum_fusion.11), channel_id=1, source_target_pairs={{0,1},{1,2},{2,3},{4,5},{5,6},{6,7},{8,9},{9,10},{10,11},{12,13},{... | collective-permute-start | bytes 55304 | tf_op jit(solution)/shard_map/ppermute | solution.py:17
  7.4 1.3 %collective-permute-start.3 = (f32[9,4,128]{2,1,0:T(4,128)S(1)}, f32[9,4,128]{2,1,0:T(4,128)S(1)}, u32[]{:S(2)}, u32[]{:S(2)}) collective-permute-start(f32[9,4,128]{2,1,0:T(4,128)S(1)} %pad_maximum_fusion.12), channel_id=1, source_target_pairs={{1,0},{2,1},{3,2},{5,4},{6,5},{7,6},{9,8},{10,9},{11,10},{13,12},{... | collective-permute-start | bytes 55304 | tf_op jit(solution)/shard_map/ppermute | solution.py:17
  8.7 4.2 %collective-permute-start = (f32[9,8,128]{2,1,0:T(8,128)S(1)}, f32[9,8,128]{2,1,0:T(8,128)S(1)}, u32[]{:S(2)}, u32[]{:S(2)}) collective-permute-start(f32[9,8,128]{2,1,0:T(8,128)S(1)} %pad_maximum_fusion.9), channel_id=1, source_target_pairs={{0,4},{4,8},{8,12},{12,16},{16,20},{20,24},{24,28},{1,5},{5,9},{9,... | collective-permute-start | bytes 110600 | tf_op jit(solution)/shard_map/ppermute | solution.py:17
  12.9 1.3 %collective-permute-start.1 = (f32[9,8,128]{2,1,0:T(8,128)S(1)}, f32[9,8,128]{2,1,0:T(8,128)S(1)}, u32[]{:S(2)}, u32[]{:S(2)}) collective-permute-start(f32[9,8,128]{2,1,0:T(8,128)S(1)} %pad_maximum_fusion.10), channel_id=1, source_target_pairs={{4,0},{8,4},{12,8},{16,12},{20,16},{24,20},{28,24},{5,1},{9,5},{13... | collective-permute-start | bytes 110600 | tf_op jit(solution)/shard_map/ppermute | solution.py:17
  14.4 0.2 fusion.12
  14.6 0.2 add.125
  14.9 0.2 sub.40
  15.1 0.1 broadcast_multiply_fusion.2
  15.2 0.1 mul.251
  15.3 0.1 mul.256
  15.5 0.4 convolution_bitcast_fusion
  15.9 0.3 reshape.170
  16.2 0.1 fusion.61
  16.3 0.2 reduce_window_sum.11
  16.5 0.3 convolution_multiply_fusion.3
  16.9 0.4 fusion.5
  17.4 0.1 add.120
  17.5 0.1 sub.38
  17.6 0.4 convolution_bitcast_fusion.1
  18.0 0.1 reshape.169
  18.2 0.6 collective-permute-done.1
  18.8 0.1 add.116
  18.9 0.1 sub.36
  19.0 0.4 convolution_bitcast_fusion.2
  19.4 0.1 reshape.166
  19.6 0.1 fusion.8
  19.8 0.5 copy-done.3
  20.2 0.4 fusion.4
  20.6 0.4 fusion.65
  21.1 43.9 %psum.7 = f32[2]{0:T(128)S(1)} all-reduce(f32[2]{0:T(128)S(1)} %get-tuple-element.40), channel_id=1, replica_groups=mesh['px'=8,'py'=4] {'px','py'}, use_global_device_ids=true, to_apply=%region_2.3 | all-reduce | flops 2 | bytes 16 | tf_op jit(solution)/shard_map/psum | solution.py:171
  65.1 0.1 mul.266
  65.1 0.1 mul.267
  65.2 0.2 copy_multiply_fusion
  65.4 0.6 gather_fusion
  65.9 0.1 select_bitcast_fusion
  66.0 0.3 fusion.41
  66.4 0.7 copy.106
  67.0 3.5 %all-to-all-start = ((f32[4,4,16,128]{3,1,2,0:T(4,128)}), f32[4,4,16,128]{3,1,2,0:T(4,128)S(1)}, u32[]{:S(2)}, u32[]{:S(2)}) async-start(f32[4,4,16,128]{3,1,2,0:T(4,128)} %copy.106), calls=%async_computation | async-start | bytes 262144 | tf_op jit(solution)/shard_map/all_to_all | solution.py:190
  70.6 0.8 %broadcast_multiply_fusion = f32[2,2,2,2,4,8,128]{6,5,4,3,2,1,0:T(8,128)} fusion(f32[2,2,2,2,4,8,128]{6,5,4,3,2,1,0:T(8,128)S(1)} %bitcast.158, f32[2]{0:T(128)S(1)} %multiply_divide_fusion), kind=kLoop, calls=%fused_computation.78 | loop fusion | flops 65536 | bytes 524296 | tf_op jit(solution)/shard_map/mul | solution.py:173
  71.4 3.8 %all-to-all-done = f32[4,4,16,128]{3,1,2,0:T(4,128)S(1)} async-done(((f32[4,4,16,128]{3,1,2,0:T(4,128)}), f32[4,4,16,128]{3,1,2,0:T(4,128)S(1)}, u32[]{:S(2)}, u32[]{:S(2)}) %all-to-all-start) | async-done | bytes 131104 | tf_op jit(solution)/shard_map/all_to_all | solution.py:190
  75.2 0.7 copy.107
  (70 shorter events, 0.7 us)
Async XLA Ops:
  1.7 1.6 %copy-start.6 = (f32[8,8]{1,0:T(8,128)S(1)}, f32[8,8]{1,0:T(8,128)}, u32[]{:S(2)}) copy-start(f32[8,8]{1,0:T(8,128)} %constant.61.clone) | copy-start | bytes 772
  1.7 1.9 %copy-start.8 = (f32[8,81]{1,0:T(8,128)S(1)}, f32[8,81]{1,0:T(8,128)}, u32[]{:S(2)}) copy-start(f32[8,81]{1,0:T(8,128)} %constant.62.clone) | copy-start | bytes 7780
  3.2 1.1 %copy-start.7 = (f32[8,8]{1,0:T(8,128)S(1)}, f32[8,8]{1,0:T(8,128)}, u32[]{:S(2)}) copy-start(f32[8,8]{1,0:T(8,128)} %constant.64.clone) | copy-start | bytes 772
  3.3 1.4 %copy-start = (f32[3,3,3,3,4,8,128]{6,5,4,3,2,1,0:T(8,128)S(1)}, f32[3,3,3,3,4,8,128]{6,5,4,3,2,1,0:T(8,128)}, u32[]{:S(2)}) copy-start(f32[3,3,3,3,4,8,128]{6,5,4,3,2,1,0:T(8,128)} %param.12) | copy-start | bytes 3981316
  4.8 9.5 %copy-start.10 = (s32[1,8]{1,0:T(1,128)S(1)}, s32[1,8]{1,0:T(1,128)}, u32[]{:S(2)}) copy-start(s32[1,8]{1,0:T(1,128)} %param.14) | copy-start | bytes 100
  4.9 12.3 %collective-permute-start.2 = (f32[9,4,128]{2,1,0:T(4,128)S(1)}, f32[9,4,128]{2,1,0:T(4,128)S(1)}, u32[]{:S(2)}, u32[]{:S(2)}) collective-permute-start(f32[9,4,128]{2,1,0:T(4,128)S(1)} %pad_maximum_fusion.11), channel_id=1, source_target_pairs={{0,1},{1,2},{2,3},{4,5},{5,6},{6,7},{8,9},{9,10},{10,11},{12,13},{... | collective-permute-start | bytes 55304 | tf_op jit(solution)/shard_map/ppermute | solution.py:17
  7.4 9.9 %collective-permute-start.3 = (f32[9,4,128]{2,1,0:T(4,128)S(1)}, f32[9,4,128]{2,1,0:T(4,128)S(1)}, u32[]{:S(2)}, u32[]{:S(2)}) collective-permute-start(f32[9,4,128]{2,1,0:T(4,128)S(1)} %pad_maximum_fusion.12), channel_id=1, source_target_pairs={{1,0},{2,1},{3,2},{5,4},{6,5},{7,6},{9,8},{10,9},{11,10},{13,12},{... | collective-permute-start | bytes 55304 | tf_op jit(solution)/shard_map/ppermute | solution.py:17
  8.7 9.4 %collective-permute-start = (f32[9,8,128]{2,1,0:T(8,128)S(1)}, f32[9,8,128]{2,1,0:T(8,128)S(1)}, u32[]{:S(2)}, u32[]{:S(2)}) collective-permute-start(f32[9,8,128]{2,1,0:T(8,128)S(1)} %pad_maximum_fusion.9), channel_id=1, source_target_pairs={{0,4},{4,8},{8,12},{12,16},{16,20},{20,24},{24,28},{1,5},{5,9},{9,... | collective-permute-start | bytes 110600 | tf_op jit(solution)/shard_map/ppermute | solution.py:17
  12.9 5.9 %collective-permute-start.1 = (f32[9,8,128]{2,1,0:T(8,128)S(1)}, f32[9,8,128]{2,1,0:T(8,128)S(1)}, u32[]{:S(2)}, u32[]{:S(2)}) collective-permute-start(f32[9,8,128]{2,1,0:T(8,128)S(1)} %pad_maximum_fusion.10), channel_id=1, source_target_pairs={{4,0},{8,4},{12,8},{16,12},{20,16},{24,20},{28,24},{5,1},{9,5},{13... | collective-permute-start | bytes 110600 | tf_op jit(solution)/shard_map/ppermute | solution.py:17
  14.3 1.2 %copy-start.1 = (f32[4,4,1]{1,0,2:T(4,128)S(1)}, f32[4,4,1]{1,0,2:T(4,128)}, u32[]{:S(2)}) copy-start(f32[4,4,1]{1,0,2:T(4,128)} %constant.86) | copy-start | bytes 196
  14.4 1.9 %copy-start.9 = (s32[1,8,1]{1,2,0:T(1,128)S(1)}, s32[1,8,1]{1,2,0:T(1,128)}, u32[]{:S(2)}) copy-start(s32[1,8,1]{1,2,0:T(1,128)} %param.15) | copy-start | bytes 100
  14.6 1.9 %copy-start.5 = (f32[8,8,1]{1,0,2:T(8,128)S(1)}, f32[8,8,1]{1,0,2:T(8,128)}, u32[]{:S(2)}) copy-start(f32[8,8,1]{1,0,2:T(8,128)} %constant.83) | copy-start | bytes 772
  14.9 2.0 %copy-start.4 = (f32[8,8,1]{1,0,2:T(8,128)S(1)}, f32[8,8,1]{1,0,2:T(8,128)}, u32[]{:S(2)}) copy-start(f32[8,8,1]{1,0,2:T(8,128)} %constant.84) | copy-start | bytes 772
  19.5 0.7 copy-start.3
  19.6 1.0 %copy-start.2 = (f32[8,8,1]{1,0,2:T(8,128)S(1)}, f32[8,8,1]{1,0,2:T(8,128)}, u32[]{:S(2)}) copy-start(f32[8,8,1]{1,0,2:T(8,128)} %constant.87) | copy-start | bytes 772
  19.7 45.4 %copy-start.11 = (f32[2]{0:T(128)S(1)}, f32[2]{0:T(128)}, u32[]{:S(2)}) copy-start(f32[2]{0:T(128)} %param.13) | copy-start | bytes 28
  67.0 8.1 %all-to-all-start = ((f32[4,4,16,128]{3,1,2,0:T(4,128)}), f32[4,4,16,128]{3,1,2,0:T(4,128)S(1)}, u32[]{:S(2)}, u32[]{:S(2)}) async-start(f32[4,4,16,128]{3,1,2,0:T(4,128)} %copy.106), calls=%async_computation | async-start | bytes 262144 | tf_op jit(solution)/shard_map/all_to_all | solution.py:190
where the time goes:
time: 76.3 us; the launch traced here: 75.8 us
  blocking collectives  43.9 us (58%)
  starting transfers between devices  12.7 us (17%)
  local copies, waits for them, and re-layouts  6.92 us (9%)
  waiting for transfers between devices  4.44 us (6%)
  matrix products  4.35 us (6%)
  other arithmetic  2.08 us (3%)
  between operations  1.39 us (2%)
    psum x1, blocking collectives, body(): totals = lax.psum(jnp.sum(remapped.reshape(2, -1), axis=1), ('px', 'py'))  43.9 us
    ppermute x4, starting transfers between devices, passed_along(): return lax.ppermute(x, axis, pairs)  9.2 us
    all_to_all x1, waiting for transfers between devices, body(): lax.all_to_all(send_rows, 'py', split_axis=0, concat_axis=0, tiled=True)  3.81 us
    all_to_all x1, starting transfers between devices, body(): lax.all_to_all(send_rows, 'py', split_axis=0, concat_axis=0, tiled=True)  3.54 us
    reshape x1, local copies, waits for them, and re-layouts, lagrange_section(): node_motion = velocity.reshape(81, zone_count)  1.54 us
  transfers between devices with their start and end apart: 5, of which 2 were waited for; matrix products, arithmetic and copies ran while one was open for 6% of the time, Pallas kernels for 0%

commit v1 on v0

--- a/solution.py
+++ b/solution.py
@@ -168,7 +168,7 @@
     motion_y = jnp.concatenate([below_y[8][:, None], relative[1], above_y[8][:, None]], axis=1)
     y_faces = (left_y, right_y, 0.5 * (motion_y[:, :-1] + motion_y[:, 1:]))
     remapped = advect(lagrange, relative, x_faces, y_faces, tables)
-    totals = lax.psum(jnp.sum(remapped.reshape(2, -1), axis=1), ("px", "py"))
+    totals = jnp.sum(lax.all_gather(jnp.sum(remapped.reshape(2, -1), axis=1), ("px", "py")), axis=0)
     field_means = totals / total_zones
     fixed_state = remapped * (targets / field_means).reshape(2, 1, 1, 1, 1, 1, 1)
     entries = handoff_blocks.shape[1]

time: 76.3 us -> 76.6 us (level)
    psum x1 -> x0, blocking collectives: 43.9 us -> none  [body(): totals = lax.psum(jnp.sum(remapped.reshape(2, -1), axis=1), ('px', 'py'))]
    unnamed x0 -> x1, blocking collectives: none -> 43.9 us
where the time goes in v1:
time: 76.6 us; the launch traced here: 76.2 us
  blocking collectives  43.9 us (57%)
  starting transfers between devices  12.7 us (17%)
  local copies, waits for them, and re-layouts  7.25 us (9%)
  waiting for transfers between devices  4.43 us (6%)
  matrix products  4.35 us (6%)
  other arithmetic  2.1 us (3%)
  between operations  1.42 us (2%)
    unnamed x1, blocking collectives  43.9 us
    ppermute x4, starting transfers between devices, passed_along(): return lax.ppermute(x, axis, pairs)  9.2 us
    all_to_all x1, waiting for transfers between devices, body(): lax.all_to_all(send_rows, 'py', split_axis=0, concat_axis=0, tiled=True)  3.81 us
    all_to_all x1, starting transfers between devices, body(): lax.all_to_all(send_rows, 'py', split_axis=0, concat_axis=0, tiled=True)  3.54 us
    reshape x1, local copies, waits for them, and re-layouts, lagrange_section(): node_motion = velocity.reshape(81, zone_count)  1.54 us
  transfers between devices with their start and end apart: 5, of which 2 were waited for; matrix products, arithmetic and copies ran while one was open for 6% of the time, Pallas kernels for 0%

profile of v1, /device:TPU:0, one launch (start us, length us, event | category | flops | bytes accessed | tf_op | source)
XLA Modules:
  0.0 76.2 jit_solution(15084756391232173261)
XLA Ops:
  0.6 1.0 %fusion.62 = (f32[1,2,2,2,4,8,128]{6,5,4,3,2,1,0:T(8,128)S(1)}, f32[1,2,2,2,4,8,128]{6,5,4,3,2,1,0:T(8,128)S(1)}) fusion(f32[2,2,2,2,4,8,128]{6,5,4,3,2,1,0:T(8,128)} %param.11), kind=kLoop, calls=%fused_computation.139 | loop fusion | bytes 524288 | tf_op jit(solution)/shard_map/slice | solution.py:90
  1.7 1.5 %reshape.163 = f32[81,4096]{1,0:T(8,128)S(1)} reshape(f32[3,3,3,3,4,8,128]{6,5,4,3,2,1,0:T(8,128)} %param.12) | data formatting | bytes 2654208 | tf_op jit(solution)/shard_map/reshape | solution.py:87
  3.3 0.3 convolution_multiply_fusion.6
  3.5 0.8 %convolution_multiply_fusion.5 = f32[8,4096]{1,0:T(8,128)S(1)} fusion(f32[8,4096]{1,0:T(8,128)S(1)} %convolution_multiply_fusion.6, f32[8,81]{1,0:T(8,128)S(1)} %copy-done.8, f32[81,4096]{1,0:T(8,128)S(1)} %reshape.163), kind=kOutput, calls=%fused_computation.17 | convolution fusion | flops 31883264 | bytes 1591840 | tf_op jit(solution)/shard_map/dot_general | solution.py:88
  4.3 0.3 fusion.7
  4.6 0.1 reduce_sum.36
  4.7 0.1 fusion.46
  4.9 2.4 %collective-permute-start.2 = (f32[9,4,128]{2,1,0:T(4,128)S(1)}, f32[9,4,128]{2,1,0:T(4,128)S(1)}, u32[]{:S(2)}, u32[]{:S(2)}) collective-permute-start(f32[9,4,128]{2,1,0:T(4,128)S(1)} %pad_maximum_fusion.11), channel_id=1, source_target_pairs={{0,1},{1,2},{2,3},{4,5},{5,6},{6,7},{8,9},{9,10},{10,11},{12,13},{... | collective-permute-start | bytes 55304 | tf_op jit(solution)/shard_map/ppermute | solution.py:17
  7.4 1.3 %collective-permute-start.3 = (f32[9,4,128]{2,1,0:T(4,128)S(1)}, f32[9,4,128]{2,1,0:T(4,128)S(1)}, u32[]{:S(2)}, u32[]{:S(2)}) collective-permute-start(f32[9,4,128]{2,1,0:T(4,128)S(1)} %pad_maximum_fusion.12), channel_id=1, source_target_pairs={{1,0},{2,1},{3,2},{5,4},{6,5},{7,6},{9,8},{10,9},{11,10},{13,12},{... | collective-permute-start | bytes 55304 | tf_op jit(solution)/shard_map/ppermute | solution.py:17
  8.7 4.2 %collective-permute-start = (f32[9,8,128]{2,1,0:T(8,128)S(1)}, f32[9,8,128]{2,1,0:T(8,128)S(1)}, u32[]{:S(2)}, u32[]{:S(2)}) collective-permute-start(f32[9,8,128]{2,1,0:T(8,128)S(1)} %pad_maximum_fusion.9), channel_id=1, source_target_pairs={{0,4},{4,8},{8,12},{12,16},{16,20},{20,24},{24,28},{1,5},{5,9},{9,... | collective-permute-start | bytes 110600 | tf_op jit(solution)/shard_map/ppermute | solution.py:17
  12.9 1.3 %collective-permute-start.1 = (f32[9,8,128]{2,1,0:T(8,128)S(1)}, f32[9,8,128]{2,1,0:T(8,128)S(1)}, u32[]{:S(2)}, u32[]{:S(2)}) collective-permute-start(f32[9,8,128]{2,1,0:T(8,128)S(1)} %pad_maximum_fusion.10), channel_id=1, source_target_pairs={{4,0},{8,4},{12,8},{16,12},{20,16},{24,20},{28,24},{5,1},{9,5},{13... | collective-permute-start | bytes 110600 | tf_op jit(solution)/shard_map/ppermute | solution.py:17
  14.4 0.2 fusion.12
  14.6 0.2 add.123
  14.9 0.2 sub.40
  15.1 0.1 broadcast_multiply_fusion.2
  15.2 0.1 mul.251
  15.3 0.1 mul.256
  15.5 0.4 convolution_bitcast_fusion
  15.9 0.3 reshape.170
  16.2 0.1 fusion.61
  16.3 0.2 reduce_window_sum.11
  16.5 0.3 convolution_multiply_fusion.3
  16.9 0.4 fusion.5
  17.6 0.4 convolution_bitcast_fusion.1
  18.0 0.1 reshape.169
  18.2 0.6 collective-permute-done.1
  18.8 0.1 add.114
  18.9 0.1 sub.36
  19.0 0.4 convolution_bitcast_fusion.2
  19.4 0.1 reshape.166
  19.6 0.1 fusion.8
  19.8 0.5 copy-done.3
  20.2 0.4 fusion.4
  20.6 0.4 fusion.65
  21.1 0.2 dynamic-update-slice
  21.4 43.9 %all-reduce.3 = f32[64]{0:T(128)S(1)} all-reduce(f32[64]{0:T(128)S(1)} %dynamic-update-slice), channel_id=2, replica_groups=mesh['px'=8,'py'=4] {'px','py'}, use_global_device_ids=true, to_apply=%add.3 | all-reduce | flops 64 | bytes 512
  65.2 0.1 reshape.183
  65.4 0.1 mul.266
  65.5 0.1 mul.267
  65.6 0.2 copy_multiply_fusion
  65.7 0.6 gather_fusion
  66.3 0.1 select_bitcast_fusion
  66.4 0.3 fusion.41
  66.7 0.7 copy.106
  67.4 3.5 %all-to-all-start = ((f32[4,4,16,128]{3,1,2,0:T(4,128)}), f32[4,4,16,128]{3,1,2,0:T(4,128)S(1)}, u32[]{:S(2)}, u32[]{:S(2)}) async-start(f32[4,4,16,128]{3,1,2,0:T(4,128)} %copy.106), calls=%async_computation | async-start | bytes 262144 | tf_op jit(solution)/shard_map/all_to_all | solution.py:190
  70.9 0.8 %broadcast_multiply_fusion = f32[2,2,2,2,4,8,128]{6,5,4,3,2,1,0:T(8,128)} fusion(f32[2,2,2,2,4,8,128]{6,5,4,3,2,1,0:T(8,128)S(1)} %bitcast.158, f32[2]{0:T(128)S(1)} %multiply_divide_fusion), kind=kLoop, calls=%fused_computation.78 | loop fusion | flops 65536 | bytes 524296 | tf_op jit(solution)/shard_map/mul | solution.py:173
  71.7 3.8 %all-to-all-done = f32[4,4,16,128]{3,1,2,0:T(4,128)S(1)} async-done(((f32[4,4,16,128]{3,1,2,0:T(4,128)}), f32[4,4,16,128]{3,1,2,0:T(4,128)S(1)}, u32[]{:S(2)}, u32[]{:S(2)}) %all-to-all-start) | async-done | bytes 131104 | tf_op jit(solution)/shard_map/all_to_all | solution.py:190
  75.5 0.7 copy.107
  (74 shorter events, 0.9 us)
Async XLA Ops:
  1.7 1.6 %copy-start.6 = (f32[8,8]{1,0:T(8,128)S(1)}, f32[8,8]{1,0:T(8,128)}, u32[]{:S(2)}) copy-start(f32[8,8]{1,0:T(8,128)} %constant.61.clone) | copy-start | bytes 772
  1.7 1.9 %copy-start.8 = (f32[8,81]{1,0:T(8,128)S(1)}, f32[8,81]{1,0:T(8,128)}, u32[]{:S(2)}) copy-start(f32[8,81]{1,0:T(8,128)} %constant.62.clone) | copy-start | bytes 7780
  3.2 1.1 %copy-start.7 = (f32[8,8]{1,0:T(8,128)S(1)}, f32[8,8]{1,0:T(8,128)}, u32[]{:S(2)}) copy-start(f32[8,8]{1,0:T(8,128)} %constant.64.clone) | copy-start | bytes 772
  3.3 1.4 %copy-start = (f32[3,3,3,3,4,8,128]{6,5,4,3,2,1,0:T(8,128)S(1)}, f32[3,3,3,3,4,8,128]{6,5,4,3,2,1,0:T(8,128)}, u32[]{:S(2)}) copy-start(f32[3,3,3,3,4,8,128]{6,5,4,3,2,1,0:T(8,128)} %param.12) | copy-start | bytes 3981316
  4.8 9.5 %copy-start.10 = (s32[1,8]{1,0:T(1,128)S(1)}, s32[1,8]{1,0:T(1,128)}, u32[]{:S(2)}) copy-start(s32[1,8]{1,0:T(1,128)} %param.14) | copy-start | bytes 100
  4.9 12.4 %collective-permute-start.2 = (f32[9,4,128]{2,1,0:T(4,128)S(1)}, f32[9,4,128]{2,1,0:T(4,128)S(1)}, u32[]{:S(2)}, u32[]{:S(2)}) collective-permute-start(f32[9,4,128]{2,1,0:T(4,128)S(1)} %pad_maximum_fusion.11), channel_id=1, source_target_pairs={{0,1},{1,2},{2,3},{4,5},{5,6},{6,7},{8,9},{9,10},{10,11},{12,13},{... | collective-permute-start | bytes 55304 | tf_op jit(solution)/shard_map/ppermute | solution.py:17
  7.4 10.0 %collective-permute-start.3 = (f32[9,4,128]{2,1,0:T(4,128)S(1)}, f32[9,4,128]{2,1,0:T(4,128)S(1)}, u32[]{:S(2)}, u32[]{:S(2)}) collective-permute-start(f32[9,4,128]{2,1,0:T(4,128)S(1)} %pad_maximum_fusion.12), channel_id=1, source_target_pairs={{1,0},{2,1},{3,2},{5,4},{6,5},{7,6},{9,8},{10,9},{11,10},{13,12},{... | collective-permute-start | bytes 55304 | tf_op jit(solution)/shard_map/ppermute | solution.py:17
  8.7 9.5 %collective-permute-start = (f32[9,8,128]{2,1,0:T(8,128)S(1)}, f32[9,8,128]{2,1,0:T(8,128)S(1)}, u32[]{:S(2)}, u32[]{:S(2)}) collective-permute-start(f32[9,8,128]{2,1,0:T(8,128)S(1)} %pad_maximum_fusion.9), channel_id=1, source_target_pairs={{0,4},{4,8},{8,12},{12,16},{16,20},{20,24},{24,28},{1,5},{5,9},{9,... | collective-permute-start | bytes 110600 | tf_op jit(solution)/shard_map/ppermute | solution.py:17
  12.9 5.9 %collective-permute-start.1 = (f32[9,8,128]{2,1,0:T(8,128)S(1)}, f32[9,8,128]{2,1,0:T(8,128)S(1)}, u32[]{:S(2)}, u32[]{:S(2)}) collective-permute-start(f32[9,8,128]{2,1,0:T(8,128)S(1)} %pad_maximum_fusion.10), channel_id=1, source_target_pairs={{4,0},{8,4},{12,8},{16,12},{20,16},{24,20},{28,24},{5,1},{9,5},{13... | collective-permute-start | bytes 110600 | tf_op jit(solution)/shard_map/ppermute | solution.py:17
  14.3 1.2 %copy-start.1 = (f32[4,4,1]{1,0,2:T(4,128)S(1)}, f32[4,4,1]{1,0,2:T(4,128)}, u32[]{:S(2)}) copy-start(f32[4,4,1]{1,0,2:T(4,128)} %constant.90) | copy-start | bytes 196
  14.4 1.9 %copy-start.9 = (s32[1,8,1]{1,2,0:T(1,128)S(1)}, s32[1,8,1]{1,2,0:T(1,128)}, u32[]{:S(2)}) copy-start(s32[1,8,1]{1,2,0:T(1,128)} %param.15) | copy-start | bytes 100
  14.6 1.9 %copy-start.5 = (f32[8,8,1]{1,0,2:T(8,128)S(1)}, f32[8,8,1]{1,0,2:T(8,128)}, u32[]{:S(2)}) copy-start(f32[8,8,1]{1,0,2:T(8,128)} %constant.87) | copy-start | bytes 772
  14.9 2.0 %copy-start.4 = (f32[8,8,1]{1,0,2:T(8,128)S(1)}, f32[8,8,1]{1,0,2:T(8,128)}, u32[]{:S(2)}) copy-start(f32[8,8,1]{1,0,2:T(8,128)} %constant.88) | copy-start | bytes 772
  19.5 0.7 copy-start.3
  19.6 1.0 %copy-start.2 = (f32[8,8,1]{1,0,2:T(8,128)S(1)}, f32[8,8,1]{1,0,2:T(8,128)}, u32[]{:S(2)}) copy-start(f32[8,8,1]{1,0,2:T(8,128)} %constant.91) | copy-start | bytes 772
  19.7 45.7 %copy-start.11 = (f32[2]{0:T(128)S(1)}, f32[2]{0:T(128)}, u32[]{:S(2)}) copy-start(f32[2]{0:T(128)} %param.13) | copy-start | bytes 28
  67.4 8.1 %all-to-all-start = ((f32[4,4,16,128]{3,1,2,0:T(4,128)}), f32[4,4,16,128]{3,1,2,0:T(4,128)S(1)}, u32[]{:S(2)}, u32[]{:S(2)}) async-start(f32[4,4,16,128]{3,1,2,0:T(4,128)} %copy.106), calls=%async_computation | async-start | bytes 262144 | tf_op jit(solution)/shard_map/all_to_all | solution.py:190
